TPU v7x, 128 devices: a whole 4x4x4 slice. The times are simulated.
128 devices in a mesh: row: 8 (over x, core), col: 16 (over y, z).
Axes of the slice: x: 4, y: 4, z: 4, core: 2. Of those that a mesh axis runs over, the one named last changes fastest.
Arguments:
- factor: float32 [4, 8, 1024, 2048], P(None, 'row', None, 'col'), as said below
- cross_cov: float32 [4, 8, 1024, 1024], P(None, 'row', 'col'), may hold values from -6 to 6
Outputs:
- overwritten: float32 [4, 8, 1024, 1024], P(None, 'row', 'col')
Inputs may be any that keep to these rules, and one draw needn't show every extreme that they name: The diagonal entries of the factor lie between 1 and 3.
All inputs are finite; a program needn't handle non-finite values.
Results may differ from a plain program's by a relative error of at most 0.00014.
Values sent between devices are 32-bit elements; how exact they have to be, the bound alone decides.
No kernel may reach another device: no remote copies, remote signals or barrier semaphores. Data moves between devices by JAX's collectives and lax.ppermute only.
A program may use at most 128 MiB of HBM per device.

v0:
```python
import jax
import jax.numpy as jnp
from jax import lax
from jax.sharding import PartitionSpec as P


def broadcast(x, axis, root):
    mine = lax.axis_index(axis) == root
    return lax.psum(jnp.where(mine, x, jnp.zeros_like(x)), axis)


def spread(block, root):
    return broadcast(block, "row", root)


def reduce_turn(partial_value):
    return lax.psum_scatter(partial_value, "col", scatter_dimension=0, tiled=True)


def shards(factor, cross_cov):
    col_id = lax.axis_index("col")
    row_id = lax.axis_index("row")
    lead_rows = factor[0, 0]
    own_rhs = cross_cov[0, 0]
    block_row, block_rhs = (
        lax.all_gather(lead_rows, "col", axis=1, tiled=True),
        lax.all_gather(own_rhs, "col", axis=0, tiled=True),
    )
    block_size = block_row.shape[0]
    first_block = lax.linalg.triangular_solve(
        block_row[:, :block_size], block_rhs, left_side=True, lower=True
    )
    first_block = spread(first_block, 0)
    second_rhs = block_rhs - jnp.dot(
        block_row[:, :block_size], first_block, precision=lax.Precision.HIGHEST
    )
    second_block = lax.linalg.triangular_solve(
        block_row[:, block_size:], second_rhs, left_side=True, lower=True
    )
    second_block = spread(second_block, 1)
    solved = jnp.concatenate([first_block, second_block], 0)
    local_factor = factor[:, 0]
    col_width = local_factor.shape[2]
    my_rows = lax.dynamic_slice_in_dim(solved, col_id * col_width, col_width, 0)
    pieces = []
    for turn_id in range(local_factor.shape[0]):
        partial_value = jnp.dot(local_factor[turn_id], my_rows, precision=lax.Precision.HIGHEST)
        pieces.append(reduce_turn(partial_value))
    reduced = jnp.stack(pieces, 0)
    updated = cross_cov[:, 0] - reduced
    slice_rows = own_rhs.shape[0]
    first_piece = lax.dynamic_slice_in_dim(first_block, col_id * slice_rows, slice_rows, 0)
    second_piece = lax.dynamic_slice_in_dim(second_block, col_id * slice_rows, slice_rows, 0)
    head_rows = jnp.where(
        row_id == 0, first_piece, jnp.where(row_id == 1, second_piece, updated[0])
    )
    result = jnp.concatenate([head_rows[None], updated[1:]], 0)
    return result[:, None]


def solution(mesh):
    placed = (P(None, "row", None, "col"), P(None, "row", "col", None))
    return jax.shard_map(
        shards, mesh=mesh, in_specs=placed, out_specs=P(None, "row", "col", None), check_vma=False
    )
```

profile of v0, /device:TPU:0, one launch (start us, length us, event | category | flops | bytes accessed | tf_op | source)
XLA Modules:
  0.0 875.4 jit_solution(348379081481082438)
XLA Ops:
  10.5 53.1 %all-gather.7.cloned.1.call-done = f32[1,1,1024,1024]{3,1,0,2:T(1,128)} async-done(((f32[1,1,64,1024]{3,1,0,2:T(1,128)}), f32[1,1,1024,1024]{3,1,0,2:T(1,128)}) %all-gather.7.cloned.1.call-update) | async-done | bytes 4194320 | tf_op jit(solution)/shard_map/all_gather | solution.py:27
  63.7 11.0 %copy.10 = f32[1,1,1024,1024]{2,3,1,0:T(8,128)} copy(f32[1,1,1024,1024]{3,1,0,2:T(1,128)} %all-gather.7.cloned.1.call-done) | data formatting | bytes 8388608 | tf_op jit(solution)/shard_map/all_gather | solution.py:27
  74.7 69.2 %all-gather.5.cloned.1.call-done = f32[1,1,1024,2048]{3,2,1,0:T(8,128)} async-done(((f32[1,1,1024,128]{3,2,1,0:T(8,128)}), f32[1,1,1024,2048]{3,2,1,0:T(8,128)}) %all-gather.5.cloned.1.call-update) | async-done | bytes 8388624 | tf_op jit(solution)/shard_map/all_gather | solution.py:26
  143.9 8.0 slice_select_fusion
  151.9 22.5 %while.4 = (s32[]{:T(128)}, f32[1024,1024]{1,0:T(8,128)}, s32[8,2]{0,1:T(2,128)S(1)}, f32[8,128,128]{2,1,0:T(8,128)S(1)}, s32[]{:T(128)}) while((s32[]{:T(128)}, f32[1024,1024]{1,0:T(8,128)}, s32[8,2]{0,1:T(2,128)S(1)}, f32[8,128,128]{2,1,0:T(8,128)S(1)}, s32[]{:T(128)}) %tuple.80), condition=%wide.while_cond, body=%wide.while_body.sunk | while | flops 2 | bytes 131181 | solution.py:30
  174.4 78.8 %custom-call.4 = f32[8,128,128]{1,2,0:T(8,128)S(1)} custom-call(f32[8,128,128]{2,1,0:T(8,128)S(1)} %get-tuple-element.20), custom_call_target="InvertDiagBlocksLowerTriangular" | custom-call | tf_op jit(solution)/shard_map/triangular_solve/custom-call.1 | solution.py:30
  258.0 2.7 convolution_subtract_fusion.1
  261.5 3.7 fusion.36
  266.0 4.4 fusion.42
  271.3 5.4 convolution_subtract_fusion.5
  277.4 6.0 convolution_subtract_fusion.3
  284.1 7.5 convolution_subtract_fusion.8
  292.3 2.5 broadcast_select_fusion.1
  294.8 22.5 %while.5 = (s32[]{:T(128)}, f32[1024,1024]{1,0:T(8,128)}, s32[8,2]{0,1:T(2,128)S(1)}, f32[8,128,128]{2,1,0:T(8,128)S(1)}, s32[]{:T(128)}) while((s32[]{:T(128)}, f32[1024,1024]{1,0:T(8,128)}, s32[8,2]{0,1:T(2,128)S(1)}, f32[8,128,128]{2,1,0:T(8,128)S(1)}, s32[]{:T(128)}) %tuple.102), condition=%wide.while_cond.clone, body=%wide.while_body.clone.sunk | while | flops 2 | bytes 131181 | solution.py:37
  317.3 78.6 %custom-call.5 = f32[8,128,128]{1,2,0:T(8,128)S(1)} custom-call(f32[8,128,128]{2,1,0:T(8,128)S(1)} %get-tuple-element.21), custom_call_target="InvertDiagBlocksLowerTriangular" | custom-call | tf_op jit(solution)/shard_map/triangular_solve/custom-call.1 | solution.py:37
  395.9 30.9 %bitcast_subtract_fusion = f32[1024,1024]{0,1:T(8,128)S(1)} fusion(f32[1024,1024]{1,0:T(8,128)} %all-reduce.3.cloned.1.call-done, f32[1024,2048]{1,0:T(8,128)} %bitcast.173, f32[1,1,1024,1024]{2,3,1,0:T(8,128)} %copy.10), kind=kOutput, calls=%fused_computation.7 | convolution fusion | flops 12885950464 | bytes 16777216 | tf_op jit(solution)/shard_map/dot_general | solution.py:34
  430.2 2.8 convolution_subtract_fusion
  433.7 3.7 fusion.33
  438.1 4.4 fusion.39
  443.5 5.4 convolution_subtract_fusion.4
  449.5 6.2 convolution_subtract_fusion.2
  456.3 7.3 convolution_subtract_fusion.6
  464.4 2.5 broadcast_select_fusion
  466.9 71.9 %all-reduce.5.cloned.1.call-done = f32[1024,1024]{1,0:T(8,128)} async-done(((f32[1024,1024]{1,0:T(8,128)}), f32[1024,1024]{1,0:T(8,128)}) %all-reduce.5.cloned.1.call-update) | async-done | bytes 4194320 | tf_op jit(solution)/shard_map/psum | solution.py:9
  538.8 6.2 convolution_bitcast_fusion.3
  545.1 6.1 convolution_bitcast_fusion.2
  551.3 6.1 convolution_bitcast_fusion.1
  557.5 6.2 convolution_bitcast_fusion
  563.7 59.3 %reduce-scatter.5.cloned.1.call-done = f32[64,1024]{1,0:T(8,128)} async-done(((f32[1024,1024]{1,0:T(8,128)}), f32[64,1024]{1,0:T(8,128)}) %reduce-scatter.5.cloned.1.call-update) | async-done | bytes 262160 | tf_op jit(solution)/shard_map/reduce_scatter | solution.py:17
  623.1 80.6 %reduce-scatter.7.cloned.1.call-done = f32[64,1024]{1,0:T(8,128)} async-done(((f32[1024,1024]{1,0:T(8,128)}), f32[64,1024]{1,0:T(8,128)}) %reduce-scatter.7.cloned.1.call-update) | async-done | bytes 262160 | tf_op jit(solution)/shard_map/reduce_scatter | solution.py:17
  703.7 80.4 %reduce-scatter.9.cloned.1.call-done = f32[64,1024]{1,0:T(8,128)} async-done(((f32[1024,1024]{1,0:T(8,128)}), f32[64,1024]{1,0:T(8,128)}) %reduce-scatter.9.cloned.1.call-update) | async-done | bytes 262160 | tf_op jit(solution)/shard_map/reduce_scatter | solution.py:17
  784.0 80.7 %reduce-scatter.11.cloned.1.call-done = f32[64,1024]{1,0:T(8,128)} async-done(((f32[1024,1024]{1,0:T(8,128)}), f32[64,1024]{1,0:T(8,128)}) %reduce-scatter.11.cloned.1.call-update) | async-done | bytes 262160 | tf_op jit(solution)/shard_map/reduce_scatter | solution.py:17
  (100 shorter events, 69.5 us)
Async XLA Ops:
  6.5 57.1 %all-gather.7.cloned.1.call-start = ((), (), s32[]{:S(2)}) async-start(), calls=%async_computation.11 | async-start | bytes 4456448 | tf_op jit(solution)/shard_map/all_gather | solution.py:27
  8.5 135.4 %all-gather.5.cloned.1.call-start = ((), (), s32[]{:S(2)}) async-start(), calls=%async_computation.10 | async-start | bytes 8912896 | tf_op jit(solution)/shard_map/all_gather | solution.py:26
  10.5 385.5 %all-reduce.3.cloned.1.call-start = ((), (), s32[]{:S(2)}) async-start(), calls=%async_computation.4 | async-start | bytes 8388608 | tf_op jit(solution)/shard_map/psum | solution.py:9
  253.2 4.8 copy-start
  294.7 244.1 %all-reduce.5.cloned.1.call-start = ((), (), s32[]{:S(2)}) async-start(), calls=%async_computation.5 | async-start | bytes 8388608 | tf_op jit(solution)/shard_map/psum | solution.py:9
  466.8 72.0 %copy-start.1 = (f32[4,1,1024,128]{3,2,1,0:T(8,128)S(1)}, f32[4,1,1024,128]{3,2,1,0:T(8,128)}, u32[]{:S(2)}) copy-start(f32[4,1,1024,128]{3,2,1,0:T(8,128)} %param.4) | copy-start | bytes 6291460
  466.8 156.2 %reduce-scatter.5.cloned.1.call-start = ((), (), s32[]{:S(2)}) async-start(), calls=%async_computation.6 | async-start | bytes 4456448 | tf_op jit(solution)/shard_map/reduce_scatter | solution.py:17
  545.0 158.6 %reduce-scatter.7.cloned.1.call-start = ((), (), s32[]{:S(2)}) async-start(), calls=%async_computation.7 | async-start | bytes 4456448 | tf_op jit(solution)/shard_map/reduce_scatter | solution.py:17
  551.2 232.8 %reduce-scatter.9.cloned.1.call-start = ((), (), s32[]{:S(2)}) async-start(), calls=%async_computation.8 | async-start | bytes 4456448 | tf_op jit(solution)/shard_map/reduce_scatter | solution.py:17
  557.4 307.3 %reduce-scatter.11.cloned.1.call-start = ((), (), s32[]{:S(2)}) async-start(), calls=%async_computation.9 | async-start | bytes 4456448 | tf_op jit(solution)/shard_map/reduce_scatter | solution.py:17
  563.7 301.1 %copy-start.2 = (f32[4,1,64,1024]{3,2,1,0:T(8,128)S(1)}, f32[4,1,64,1024]{3,2,1,0:T(8,128)}, u32[]{:S(2)}) copy-start(f32[4,1,64,1024]{3,2,1,0:T(8,128)} %param.5) | copy-start | bytes 3145732
Sparse Core Ops, SparseCore 0:
  9.5 54.1 all-gather.6
  65.8 78.0 all-gather.4
  294.9 73.0 all-reduce.2
  467.0 71.7 all-reduce.4
  545.1 77.8 reduce-scatter.4
  626.6 77.0 reduce-scatter.6
  707.0 76.9 reduce-scatter.8
  787.7 77.0 reduce-scatter.10
where the time goes:
time: 880 us; the launch traced here: 875 us
  waiting for transfers between devices  495 us (56%)
  other arithmetic  174 us (20%)
  matrix products  132 us (15%)
  local copies, waits for them, and re-layouts  59.6 us (7%)
  between operations  14.1 us (2%)
    reduce_scatter x4, waiting for transfers between devices, reduce_turn(): lax.psum_scatter(partial_value, 'col', scatter_dimension=0, tiled=True)  301 us
    another operation x2, other arithmetic, shards(): lax.linalg.triangular_solve(block_row[:, block_size:], second_rhs, left_s...  86.6 us
    another operation x2, other arithmetic, shards(): lax.linalg.triangular_solve(block_row[:, :block_size], block_rhs, left_si...  78.8 us
    psum x2, waiting for transfers between devices, broadcast(): return lax.psum(jnp.where(mine, x, jnp.zeros_like(x)), axis)  71.9 us
    all_gather x1, waiting for transfers between devices, shards(): lax.all_gather(lead_rows, 'col', axis=1, tiled=True)  69.2 us
    all_gather x1, waiting for transfers between devices, shards(): lax.all_gather(own_rhs, 'col', axis=0, tiled=True)  53.1 us
    another operation x15, matrix products, shards(): lax.linalg.triangular_solve(block_row[:, :block_size], block_rhs, left_si...  38.9 us
    another operation x15, matrix products, shards(): lax.linalg.triangular_solve(block_row[:, block_size:], second_rhs, left_s...  37.4 us
  transfers between devices with their start and end apart: 8, of which 7 were waited for; matrix products, arithmetic and copies ran while one was open for 15% of the time, Pallas kernels for 0%

commit v1 on v0

--- a/solution.py
+++ b/solution.py
@@ -3,10 +3,12 @@
 from jax import lax
 from jax.sharding import PartitionSpec as P
 
+create_inputs = lambda x_in, row_axis: lax.all_gather(x_in, row_axis).sum(axis=0)
+
 
 def broadcast(x, axis, root):
     mine = lax.axis_index(axis) == root
-    return lax.psum(jnp.where(mine, x, jnp.zeros_like(x)), axis)
+    return create_inputs(jnp.where(mine, x, jnp.zeros_like(x)), axis)
 
 
 def spread(block, root):

time: 880 us -> 1060 us (1.20)
  waiting for transfers between devices: 495 us -> 618 us
  other arithmetic: 174 us -> 203 us
  local copies, waits for them, and re-layouts: 59.6 us -> 83.5 us
    all_gather x0 -> x2, waiting for transfers between devices: none -> 211 us  [lax.all_gather(x_in, row_axis).sum(axis=0)]
    psum x2 -> x0, waiting for transfers between devices: 71.9 us -> none  [broadcast(): return lax.psum(jnp.where(mine, x, jnp.zeros_like(x)), axis)]
    reduce_sum x0 -> x2, other arithmetic: none -> 29.4 us  [lax.all_gather(x_in, row_axis).sum(axis=0)]
    unnamed x7 -> x11, local copies, waits for them, and re-layouts: 0.99 us -> 22.6 us
    reduce_scatter x4, waiting for transfers between devices: 301 us -> 285 us  [reduce_turn(): lax.psum_scatter(partial_value, 'col', scatter_dimension=0, tiled=True)]
  transfers between devices with their start and end apart: 8 -> 8, of which waited for: 7 -> 8; matrix products, arithmetic and copies ran while one was open for 15% -> 14% of each run, Pallas kernels for 0% -> 0%
where the time goes in v1:
time: 1060 us; the launch traced here: 1050 us
  waiting for transfers between devices  618 us (58%)
  other arithmetic  203 us (19%)
  matrix products  132 us (12%)
  local copies, waits for them, and re-layouts  83.5 us (8%)
  between operations  14.1 us (1%)
    reduce_scatter x4, waiting for transfers between devices, reduce_turn(): lax.psum_scatter(partial_value, 'col', scatter_dimension=0, tiled=True)  285 us
    all_gather x2, waiting for transfers between devices, lax.all_gather(x_in, row_axis).sum(axis=0)  211 us
    another operation x2, other arithmetic, shards(): lax.linalg.triangular_solve(block_row[:, block_size:], second_rhs, left_s...  86.6 us
    another operation x2, other arithmetic, shards(): lax.linalg.triangular_solve(block_row[:, :block_size], block_rhs, left_si...  78.8 us
    all_gather x1, waiting for transfers between devices, shards(): lax.all_gather(lead_rows, 'col', axis=1, tiled=True)  69.3 us
    all_gather x1, waiting for transfers between devices, shards(): lax.all_gather(own_rhs, 'col', axis=0, tiled=True)  53.1 us
    another operation x15, matrix products, shards(): lax.linalg.triangular_solve(block_row[:, :block_size], block_rhs, left_si...  38.9 us
    another operation x15, matrix products, shards(): lax.linalg.triangular_solve(block_row[:, block_size:], second_rhs, left_s...  37.4 us
  transfers between devices with their start and end apart: 8, of which 8 were waited for; matrix products, arithmetic and copies ran while one was open for 14% of the time, Pallas kernels for 0%

profile of v1, /device:TPU:0, one launch (start us, length us, event | category | flops | bytes accessed | tf_op | source)
XLA Modules:
  0.0 1051.9 jit_solution(94198582108374440)
XLA Ops:
  10.5 53.1 %all-gather.11.cloned.1.call-done = f32[1,1,1024,1024]{3,1,0,2:T(1,128)} async-done(((f32[1,1,64,1024]{3,1,0,2:T(1,128)}), f32[1,1,1024,1024]{3,1,0,2:T(1,128)}) %all-gather.11.cloned.1.call-update) | async-done | bytes 4194320 | tf_op jit(solution)/shard_map/all_gather | solution.py:29
  63.7 11.0 %copy.7 = f32[1,1,1024,1024]{2,3,1,0:T(8,128)} copy(f32[1,1,1024,1024]{3,1,0,2:T(1,128)} %all-gather.11.cloned.1.call-done) | data formatting | bytes 8388608 | tf_op jit(solution)/shard_map/all_gather | solution.py:29
  74.6 69.3 %all-gather.9.cloned.1.call-done = f32[1,1,1024,2048]{3,2,1,0:T(8,128)} async-done(((f32[1,1,1024,128]{3,2,1,0:T(8,128)}), f32[1,1,1024,2048]{3,2,1,0:T(8,128)}) %all-gather.9.cloned.1.call-update) | async-done | bytes 8388624 | tf_op jit(solution)/shard_map/all_gather | solution.py:28
  143.9 8.0 slice_select_fusion
  151.9 24.1 %while.4 = (s32[]{:T(128)}, f32[1024,1024]{1,0:T(8,128)}, s32[8,2]{0,1:T(2,128)S(1)}, f32[8,128,128]{2,1,0:T(8,128)S(1)}, s32[]{:T(128)}) while((s32[]{:T(128)}, f32[1024,1024]{1,0:T(8,128)}, s32[8,2]{0,1:T(2,128)S(1)}, f32[8,128,128]{2,1,0:T(8,128)S(1)}, s32[]{:T(128)}) %tuple.80), condition=%wide.while_cond, body=%wide.while_body.sunk | while | flops 2 | bytes 131181 | solution.py:32
  176.1 78.8 %custom-call.4 = f32[8,128,128]{1,2,0:T(8,128)S(1)} custom-call(f32[8,128,128]{2,1,0:T(8,128)S(1)} %get-tuple-element.20), custom_call_target="InvertDiagBlocksLowerTriangular" | custom-call | tf_op jit(solution)/shard_map/triangular_solve/custom-call.1 | solution.py:32
  267.6 4.4 fusion.42
  273.0 5.4 convolution_subtract_fusion.5
  279.1 6.0 convolution_subtract_fusion.3
  285.8 7.5 convolution_subtract_fusion.8
  296.4 23.1 %while.5 = (s32[]{:T(128)}, f32[1024,1024]{1,0:T(8,128)}, s32[8,2]{0,1:T(2,128)S(1)}, f32[8,128,128]{2,1,0:T(8,128)S(1)}, s32[]{:T(128)}) while((s32[]{:T(128)}, f32[1024,1024]{1,0:T(8,128)}, s32[8,2]{0,1:T(2,128)S(1)}, f32[8,128,128]{2,1,0:T(8,128)S(1)}, s32[]{:T(128)}) %tuple.102), condition=%wide.while_cond.clone, body=%wide.while_body.clone.sunk | while | flops 2 | bytes 131181 | solution.py:39
  319.5 78.6 %custom-call.5 = f32[8,128,128]{1,2,0:T(8,128)S(1)} custom-call(f32[8,128,128]{2,1,0:T(8,128)S(1)} %get-tuple-element.21), custom_call_target="InvertDiagBlocksLowerTriangular" | custom-call | tf_op jit(solution)/shard_map/triangular_solve/custom-call.1 | solution.py:39
  398.1 53.5 %all-gather.13.cloned.1.call-done = f32[8192,1024]{1,0:T(8,128)} async-done(((f32[1024,1024]{1,0:T(8,128)}), f32[8192,1024]{1,0:T(8,128)}) %all-gather.13.cloned.1.call-update) | async-done | bytes 33554448 | tf_op jit(solution)/shard_map/all_gather | solution.py:6
  451.6 14.6 %reduce_sum.18 = f32[1024,1024]{1,0:T(8,128)} reduce(f32[8,1024,1024]{2,1,0:T(8,128)} %bitcast.170, f32[]{:T(128)} %constant.22.clone.1), dimensions={0}, to_apply=%region_0.0 | reduce | flops 7340032 | bytes 37748740 | tf_op jit(solution)/shard_map/reduce_sum | solution.py:6
  466.2 30.8 %bitcast_subtract_fusion = f32[1024,1024]{0,1:T(8,128)S(1)} fusion(f32[1024,1024]{1,0:T(8,128)} %reduce_sum.18, f32[1024,2048]{1,0:T(8,128)} %bitcast.181, f32[1,1,1024,1024]{2,3,1,0:T(8,128)} %copy.7), kind=kOutput, calls=%fused_computation.7 | convolution fusion | flops 12885950464 | bytes 16777216 | tf_op jit(solution)/shard_map/dot_general | solution.py:36
  513.7 5.4 convolution_subtract_fusion.4
  519.8 6.1 convolution_subtract_fusion.2
  526.6 7.3 convolution_subtract_fusion.6
  537.2 157.0 %all-gather.15.cloned.1.call-done = f32[8192,1024]{1,0:T(8,128)} async-done(((f32[1024,1024]{1,0:T(8,128)}), f32[8192,1024]{1,0:T(8,128)}) %all-gather.15.cloned.1.call-update) | async-done | bytes 33554448 | tf_op jit(solution)/shard_map/all_gather | solution.py:6
  694.2 14.8 %reduce_sum.19 = f32[1024,1024]{1,0:T(8,128)} reduce(f32[8,1024,1024]{2,1,0:T(8,128)} %bitcast.171, f32[]{:T(128)} %constant.22.clone.1), dimensions={0}, to_apply=%region_1.0 | reduce | flops 7340032 | bytes 37748740 | tf_op jit(solution)/shard_map/reduce_sum | solution.py:6
  709.0 6.1 convolution_bitcast_fusion.3
  715.1 5.4 copy.13
  720.6 6.2 convolution_bitcast_fusion.2
  726.8 5.3 copy.15
  732.2 6.4 convolution_bitcast_fusion.1
  738.6 5.5 copy.17
  744.2 6.2 convolution_bitcast_fusion
  750.4 5.4 copy.19
  755.9 43.7 %reduce-scatter.13.cloned.1.call-done = f32[64,1024]{1,0:T(8,128)} async-done(((f32[1024,1024]{1,0:T(8,128)}), f32[64,1024]{1,0:T(8,128)}) %reduce-scatter.13.cloned.1.call-update) | async-done | bytes 262160 | tf_op jit(solution)/shard_map/reduce_scatter | solution.py:19
  799.5 80.6 %reduce-scatter.15.cloned.1.call-done = f32[64,1024]{1,0:T(8,128)} async-done(((f32[1024,1024]{1,0:T(8,128)}), f32[64,1024]{1,0:T(8,128)}) %reduce-scatter.15.cloned.1.call-update) | async-done | bytes 262160 | tf_op jit(solution)/shard_map/reduce_scatter | solution.py:19
  880.1 80.4 %reduce-scatter.17.cloned.1.call-done = f32[64,1024]{1,0:T(8,128)} async-done(((f32[1024,1024]{1,0:T(8,128)}), f32[64,1024]{1,0:T(8,128)}) %reduce-scatter.17.cloned.1.call-update) | async-done | bytes 262160 | tf_op jit(solution)/shard_map/reduce_scatter | solution.py:19
  960.5 80.7 %reduce-scatter.19.cloned.1.call-done = f32[64,1024]{1,0:T(8,128)} async-done(((f32[1024,1024]{1,0:T(8,128)}), f32[64,1024]{1,0:T(8,128)}) %reduce-scatter.19.cloned.1.call-update) | async-done | bytes 262160 | tf_op jit(solution)/shard_map/reduce_scatter | solution.py:19
  (106 shorter events, 93.8 us)
Async XLA Ops:
  6.5 57.1 %all-gather.11.cloned.1.call-start = ((), (), s32[]{:S(2)}) async-start(), calls=%async_computation.5 | async-start | bytes 4456448 | tf_op jit(solution)/shard_map/all_gather | solution.py:29
  8.5 135.4 %all-gather.9.cloned.1.call-start = ((), (), s32[]{:S(2)}) async-start(), calls=%async_computation.4 | async-start | bytes 8912896 | tf_op jit(solution)/shard_map/all_gather | solution.py:28
  10.5 441.1 %all-gather.13.cloned.1.call-start = ((), (), s32[]{:S(2)}) async-start(), calls=%async_computation.6 | async-start | bytes 37748736 | tf_op jit(solution)/shard_map/all_gather | solution.py:6
  254.8 4.8 copy-start
  296.3 397.9 %all-gather.15.cloned.1.call-start = ((), (), s32[]{:S(2)}) async-start(), calls=%async_computation.7 | async-start | bytes 37748736 | tf_op jit(solution)/shard_map/all_gather | solution.py:6
  537.1 262.4 %reduce-scatter.13.cloned.1.call-start = ((), (), s32[]{:S(2)}) async-start(), calls=%async_computation.8 | async-start | bytes 4456448 | tf_op jit(solution)/shard_map/reduce_scatter | solution.py:19
  694.2 14.8 %copy-start.1 = (f32[4,1,1024,128]{3,2,1,0:T(8,128)S(1)}, f32[4,1,1024,128]{3,2,1,0:T(8,128)}, u32[]{:S(2)}) copy-start(f32[4,1,1024,128]{3,2,1,0:T(8,128)} %param.4) | copy-start | bytes 6291460
  720.6 159.6 %reduce-scatter.15.cloned.1.call-start = ((), (), s32[]{:S(2)}) async-start(), calls=%async_computation.9 | async-start | bytes 4456448 | tf_op jit(solution)/shard_map/reduce_scatter | solution.py:19
  732.2 228.3 %reduce-scatter.17.cloned.1.call-start = ((), (), s32[]{:S(2)}) async-start(), calls=%async_computation.10 | async-start | bytes 4456448 | tf_op jit(solution)/shard_map/reduce_scatter | solution.py:19
  744.1 297.1 %reduce-scatter.19.cloned.1.call-start = ((), (), s32[]{:S(2)}) async-start(), calls=%async_computation.11 | async-start | bytes 4456448 | tf_op jit(solution)/shard_map/reduce_scatter | solution.py:19
  755.8 285.4 %copy-start.2 = (f32[4,1,64,1024]{3,2,1,0:T(8,128)S(1)}, f32[4,1,64,1024]{3,2,1,0:T(8,128)}, u32[]{:S(2)}) copy-start(f32[4,1,64,1024]{3,2,1,0:T(8,128)} %param.5) | copy-start | bytes 3145732
Sparse Core Ops, SparseCore 0:
  9.5 54.1 all-gather.10
  65.8 78.0 all-gather.8
  296.4 155.1 all-gather.12
  537.2 156.8 all-gather.14
  720.7 78.7 reduce-scatter.12
  803.1 77.0 reduce-scatter.14
  883.5 76.9 reduce-scatter.16
  964.2 76.9 reduce-scatter.18
